TPU v7x, 256 devices: a whole 4x4x8 slice. The times are simulated.
256 devices in a mesh: cuts: 32 (over y_lo, z, core), chan: 8 (over y_hi, x).
Axes of the slice: x: 4, y: 4 (y_hi: 2, y_lo: 2; y = y_hi * 2 + y_lo), z: 8, core: 2. Of those that a mesh axis runs over, the one named last changes fastest.
Arguments:
- data: bfloat16 [256, 384, 1024], P('cuts', None, 'chan'), may hold values from -6 to 6
- order: int32 [256], P('cuts'), may hold values from 0 to 255, as said below
- chan_factor: bfloat16 [1024, 64], P('chan'), may hold values from -0.1875 to 0.1875
- slice_weights: float32 [256, 64], P('cuts'), may hold values from 0.5 to 2
- smooth_aux: float32 [256, 384, 64], P('cuts', 'chan'), may hold values from -6 to 6
- coupled: float32 [256, 384, 64], P('cuts', 'chan'), may hold values from -6 to 6
- smooth_dual: float32 [256, 384, 64], P('cuts', 'chan'), may hold values from -2 to 2
- coupling_dual: float32 [256, 384, 64], P('cuts', 'chan'), may hold values from -2 to 2
- delta: float32 [64, 64], replicated, may hold values from -0.1125 to 1.1125, as said below
Outputs:
- evolving: float32 [256, 384, 64], P('cuts', 'chan')
- coupled_out: float32 [256, 384, 64], P('cuts', 'chan')
- delta_out: float32 [64, 64], replicated
Inputs may be any that keep to these rules, and one draw needn't show every extreme that they name: `order`: within each aligned block of 8 entries (the slices of one index of cuts) the entries are a permutation of that block's own slice indices; entry k names the stored slice of phase bin k. `delta`: A full-rank matrix.
All inputs are finite; a program needn't handle non-finite values.
Results may differ from a plain program's by a relative error of at most 0.0003.
Values sent between devices are 32-bit elements; how exact they have to be, the bound alone decides.
A program may use at most 64 MiB of HBM per device.

v0:
```python
import jax
import jax.numpy as jnp
from jax import lax
from jax.sharding import PartitionSpec as P

INNER = 3
SWEEPS = 4
POLAR = 8
smooth_weight = 1.0
eps_trace = 1e-06
highest = lax.Precision.HIGHEST


def with_halo(cells, sides, width):
    for axis, dim in sides:
        count = lax.axis_size(axis)
        head = lax.slice_in_dim(cells, 0, width, axis=dim)
        tail = lax.slice_in_dim(cells, cells.shape[dim] - width, cells.shape[dim], axis=dim)
        cells = jnp.concatenate(
            [
                lax.ppermute(tail, axis, [(i, (i + 1) % count) for i in range(count)]),
                cells,
                lax.ppermute(head, axis, [((i + 1) % count, i) for i in range(count)]),
            ],
            axis=dim,
        )
    return cells


def setup_system(slice_weights, factor_gram):
    rank = factor_gram.shape[0]
    identity = jnp.eye(rank, dtype=jnp.float32)
    diagonal_gram = jnp.diagonal(factor_gram)
    rho = jnp.sum(slice_weights * slice_weights * diagonal_gram[None, :], axis=1) / rank
    system = slice_weights[:, :, None] * factor_gram[None] * slice_weights[:, None, :]
    system = system + 2.0 * rho[:, None, None] * identity
    factors = jax.vmap(jnp.linalg.cholesky)(system)
    inverse = jax.vmap(lambda lower: jax.scipy.linalg.cho_solve((lower, True), identity))(factors)
    return (rho, inverse)


def polar_terms(gram, delta_now):
    rank = gram.shape[1]
    identity = jnp.eye(rank, dtype=jnp.float32)
    left = jnp.einsum("rs,kst->krt", delta_now, gram, precision=highest)
    normal = jnp.einsum("krt,ut->kru", left, delta_now, precision=highest)
    trace = jnp.trace(normal, axis1=1, axis2=2) + eps_trace
    current = normal / trace[:, None, None]
    root = jnp.broadcast_to(identity, normal.shape)
    for step in range(POLAR):
        bracket = 1.5 * identity - 0.5 * jnp.einsum(
            "krs,kst->krt", root, current, precision=highest
        )
        current = jnp.einsum("krs,kst->krt", current, bracket, precision=highest)
        root = jnp.einsum("krs,kst->krt", bracket, root, precision=highest)
    scale = 1.0 / jnp.sqrt(trace)
    partial_value = jnp.einsum("ksr,st->krt", root, delta_now, precision=highest)
    partial_value = (
        jnp.einsum("krt,ktu->kru", partial_value, gram, precision=highest) * scale[:, None, None]
    )
    return (root, scale, partial_value)


def coupled_update(tall, root, scale, delta_now, delta_new):
    mixer = jnp.einsum("sr,kst->krt", delta_now, root, precision=highest)
    mixer = jnp.einsum("krt,tu->kru", mixer, delta_new, precision=highest) * scale[:, None, None]
    return jnp.einsum("kir,kru->kiu", tall, mixer, precision=highest)


def smooth(aux, target, rho_cols):
    for sweep in range(SWEEPS):
        padded = with_halo(aux, (("cuts", 0),), 1)
        beside = padded[:-2] + padded[2:]
        aux = (rho_cols * target + 2.0 * smooth_weight * beside) / (rho_cols + 4.0 * smooth_weight)
    return aux


def body(
    data, order, chan_factor, slice_weights, smooth_aux, coupled, smooth_dual, coupling_dual, delta
):
    count_slices = data.shape[0]
    total_slices = count_slices * lax.axis_size("cuts")
    summed = lax.psum_scatter(
        jnp.einsum("kij,jr->ikr", data, chan_factor, preferred_element_type=jnp.float32),
        "chan",
        scatter_dimension=0,
        tiled=True,
    )
    local_order = order - lax.axis_index("cuts") * count_slices
    projected = jnp.transpose(jnp.take(summed, local_order, axis=1), (1, 0, 2))
    factor_gram = lax.psum(
        jnp.dot(chan_factor.T, chan_factor, preferred_element_type=jnp.float32), "chan"
    )
    rho, inverse = setup_system(slice_weights, factor_gram)
    data_side = projected * slice_weights[:, None, :]
    rho_cols = rho[:, None, None]
    aux = smooth_aux
    coup = coupled
    dual_s = smooth_dual
    dual_c = coupling_dual
    delta_now = delta
    evolving = aux
    for inner in range(INNER):
        rhs = data_side + rho_cols * (aux - dual_s + coup - dual_c)
        evolving = jnp.einsum("kir,krs->kis", rhs, inverse, precision=highest)
        target = evolving + dual_s
        aux = smooth(aux, target, rho_cols)
        tall = evolving + dual_c
        whole = lax.all_gather(tall, "chan", axis=1, tiled=True)
        gram = jnp.einsum("kir,kis->krs", whole, whole, precision=highest)
        root, scale, partial_value = polar_terms(gram, delta_now)
        delta_new = lax.psum(jnp.sum(partial_value, axis=0), "cuts") / total_slices
        coup = coupled_update(tall, root, scale, delta_now, delta_new)
        dual_s = dual_s + evolving - aux
        dual_c = dual_c + evolving - coup
        delta_now = delta_new
    return (evolving, coup, delta_now)


def solution(mesh):
    return jax.shard_map(
        body,
        mesh=mesh,
        in_specs=(
            P("cuts", None, "chan"),
            P("cuts"),
            P("chan", None),
            P("cuts", None),
            P("cuts", "chan", None),
            P("cuts", "chan", None),
            P("cuts", "chan", None),
            P("cuts", "chan", None),
            P(),
        ),
        out_specs=(P("cuts", "chan", None), P("cuts", "chan", None), P()),
        check_vma=False,
    )
```

profile of v0, /device:TPU:8, one launch (start us, length us, event | category | flops | bytes accessed | tf_op | source)
XLA Modules:
  0.0 663.4 jit_solution(12568983401531240565)
XLA Ops:
  7.2 0.8 fusion.184
  8.0 5.2 collective-permute-start.1
  13.2 1.1 convolution_bitcast_fusion
  14.4 1.6 copy.125
  16.2 41.4 %psum.28 = f32[64,64]{1,0:T(8,128)S(1)} all-reduce(f32[64,64]{1,0:T(8,128)S(1)} %fusion.188), channel_id=1, replica_groups=mesh['cuts'=32,'chan'=8] {'chan'}, use_global_device_ids=true, to_apply=%region_1.2 | all-reduce | flops 4096 | bytes 32768 | tf_op jit(solution)/shard_map/psum | solution.py:91
  57.6 0.8 gather_fusion.1
  58.9 46.9 %custom-call.11 = f32[8,64,64]{2,1,0:T(8,128)S(1)} custom-call(f32[8,64,64]{2,1,0:T(8,128)S(1)} %add_multiply_fusion), custom_call_target="Cholesky" | custom-call | tf_op jit(solution)/shard_map/vmap(jit(cholesky))/cholesky | solution.py:37
  106.0 39.3 %custom-call.12 = f32[8,1,64,64]{2,3,1,0:T(8,128)S(1)} custom-call(f32[8,1,64,64]{3,2,1,0:T(8,128)S(1)} %select_bitcast_fusion), custom_call_target="InvertDiagBlocksLowerTriangular" | custom-call | tf_op jit(solution)/shard_map/vmap(jit(_cho_solve))/triangular_solve | solution.py:38
  145.4 0.6 fusion.38
  146.5 1.0 copy.126
  147.4 0.6 gather_fusion
  148.1 0.5 fusion.80
  148.6 36.8 %all_gather.9 = f32[8,384,64]{2,0,1:T(8,128)S(1)} all-gather(f32[8,48,64]{2,0,1:T(8,128)S(1)} %copy.129), channel_id=1, replica_groups=mesh['cuts'=32,'chan'=8] {'chan'}, dimensions={1}, use_global_device_ids=true | all-gather | bytes 884736 | tf_op jit(solution)/shard_map/all_gather | solution.py:109
  185.5 3.0 fusion.4
  188.5 0.6 convolution_bitcast_fusion.3
  189.1 0.7 select_reduce_fusion.2
  198.7 0.5 collective-permute-start.2
  199.6 0.6 fusion.201
  201.0 3.2 collective-permute-done.2
  204.8 108.0 %psum.29 = f32[64,64]{1,0:T(8,128)S(1)} all-reduce(f32[64,64]{1,0:T(8,128)S(1)} %fusion.30), channel_id=1, replica_groups=mesh['cuts'=32,'chan'=8] {'cuts'}, use_global_device_ids=true, to_apply=%region_7.8 | all-reduce | flops 4096 | bytes 32768 | tf_op jit(solution)/shard_map/psum | solution.py:112
  313.1 0.5 collective-permute-start.6
  313.6 0.6 convolution_multiply_fusion.20
  314.6 3.9 collective-permute-done.6
  318.8 0.5 collective-permute-start.8
  319.6 0.6 collective-permute-done.9
  320.3 3.9 collective-permute-done.8
  324.8 37.0 %all_gather.10 = f32[8,384,64]{2,0,1:T(8,128)S(1)} all-gather(f32[8,48,64]{2,0,1:T(8,128)S(1)} %copy.136), channel_id=1, replica_groups=mesh['cuts'=32,'chan'=8] {'chan'}, dimensions={1}, use_global_device_ids=true | all-gather | bytes 884736 | tf_op jit(solution)/shard_map/all_gather | solution.py:109
  361.8 3.0 fusion.2
  364.8 0.6 convolution_bitcast_fusion.2
  365.4 0.7 select_reduce_fusion.1
  374.9 0.8 fusion.214
  376.2 0.5 collective-permute-start.10
  377.1 107.8 %psum.30 = f32[64,64]{1,0:T(8,128)S(1)} all-reduce(f32[64,64]{1,0:T(8,128)S(1)} %fusion.31), channel_id=1, replica_groups=mesh['cuts'=32,'chan'=8] {'cuts'}, use_global_device_ids=true, to_apply=%region_10.11 | all-reduce | flops 4096 | bytes 32768 | tf_op jit(solution)/shard_map/psum | solution.py:112
  485.2 0.5 collective-permute-start.12
  485.7 0.6 convolution_multiply_fusion.10
  486.7 3.9 collective-permute-done.12
  490.8 0.5 collective-permute-start.14
  491.7 0.6 collective-permute-done.15
  492.3 3.9 collective-permute-done.14
  496.3 1.2 fusion.187
  497.6 37.6 %all_gather.11 = f32[8,384,64]{2,0,1:T(8,128)S(1)} all-gather(f32[8,48,64]{2,0,1:T(8,128)S(1)} %copy.143), channel_id=1, replica_groups=mesh['cuts'=32,'chan'=8] {'chan'}, dimensions={1}, use_global_device_ids=true | all-gather | bytes 884736 | tf_op jit(solution)/shard_map/all_gather | solution.py:109
  535.2 3.0 fusion
  538.2 0.6 convolution_bitcast_fusion.1
  538.8 0.7 select_reduce_fusion
  548.3 0.9 fusion.227
  550.0 104.4 %psum.31 = f32[64,64]{1,0:T(8,128)S(1)} all-reduce(f32[64,64]{1,0:T(8,128)S(1)} %fusion.32), channel_id=1, replica_groups=mesh['cuts'=32,'chan'=8] {'cuts'}, use_global_device_ids=true, to_apply=%region_13.14 | all-reduce | flops 4096 | bytes 32768 | tf_op jit(solution)/shard_map/psum | solution.py:112
  654.4 0.6 convolution_multiply_fusion
  655.0 1.1 fusion.228
  (151 shorter events, 33.9 us)
Async XLA Ops:
  7.2 6.1 copy-start
  7.2 139.3 %reduce-scatter.2.cloned.1.call-start = ((), (), s32[]{:S(2)}) async-start(), calls=%async_computation.1 | async-start | bytes 1769472 | tf_op jit(solution)/shard_map/reduce_scatter | solution.py:83
  8.0 140.0 %collective-permute-start.1 = (f32[1,48,64]{2,1,0:T(8,128)S(1)}, f32[1,48,64]{2,1,0:T(8,128)S(1)}, u32[]{:S(2)}, u32[]{:S(2)}) collective-permute-start(f32[1,48,64]{2,1,0:T(8,128)S(1)} %get-tuple-element.28), channel_id=1, source_target_pairs={{8,0},{16,8},{24,16},{32,24},{40,32},{48,40},{56,48},{64,56},{72,6... | collective-permute-start | bytes 36872 | tf_op jit(solution)/shard_map/ppermute | solution.py:23
  13.2 134.8 %collective-permute-start = (f32[1,48,64]{2,1,0:T(8,128)S(1)}, f32[1,48,64]{2,1,0:T(8,128)S(1)}, u32[]{:S(2)}, u32[]{:S(2)}) collective-permute-start(f32[1,48,64]{2,1,0:T(8,128)S(1)} %get-tuple-element.27), channel_id=1, source_target_pairs={{0,8},{8,16},{16,24},{24,32},{32,40},{40,48},{48,56},{56,64},{64,7... | collective-permute-start | bytes 36872 | tf_op jit(solution)/shard_map/ppermute | solution.py:21
  14.3 1.7 copy-start.7
  16.0 42.4 %copy-start.6 = (f32[8,64]{1,0:T(8,128)S(1)}, f32[8,64]{1,0:T(8,128)}, u32[]{:S(2)}) copy-start(f32[8,64]{1,0:T(8,128)} %param.12) | copy-start | bytes 6148
  16.0 129.4 %copy-start.9 = (s32[8]{0:T(128)S(1)}, s32[8]{0:T(128)}, u32[]{:S(2)}) copy-start(s32[8]{0:T(128)} %param.10) | copy-start | bytes 100
  58.8 89.2 %copy-start.1 = (f32[8,48,64]{2,1,0:T(8,128)S(1)}, f32[8,48,64]{2,1,0:T(8,128)}, u32[]{:S(2)}) copy-start(f32[8,48,64]{2,1,0:T(8,128)} %param.13) | copy-start | bytes 294916
  58.8 89.2 %copy-start.3 = (f32[8,48,64]{2,1,0:T(8,128)S(1)}, f32[8,48,64]{2,1,0:T(8,128)}, u32[]{:S(2)}) copy-start(f32[8,48,64]{2,1,0:T(8,128)} %param.15) | copy-start | bytes 294916
  58.8 89.2 %copy-start.4 = (f32[8,48,64]{2,1,0:T(8,128)S(1)}, f32[8,48,64]{2,1,0:T(8,128)}, u32[]{:S(2)}) copy-start(f32[8,48,64]{2,1,0:T(8,128)} %param.16) | copy-start | bytes 294916
  58.8 89.2 %copy-start.5 = (f32[8,48,64]{2,1,0:T(8,128)S(1)}, f32[8,48,64]{2,1,0:T(8,128)}, u32[]{:S(2)}) copy-start(f32[8,48,64]{2,1,0:T(8,128)} %param.14) | copy-start | bytes 294916
  148.6 39.8 %copy-start.2 = (f32[64,64]{1,0:T(8,128)S(1)}, f32[64,64]{1,0:T(8,128)}, u32[]{:S(2)}) copy-start(f32[64,64]{1,0:T(8,128)} %param.17) | copy-start | bytes 49156
  198.2 2.8 collective-permute-start.3
  198.7 5.4 collective-permute-start.2
  204.3 108.6 %collective-permute-start.5 = (f32[1,48,64]{2,1,0:T(8,128)S(1)}, f32[1,48,64]{2,1,0:T(8,128)S(1)}, u32[]{:S(2)}, u32[]{:S(2)}) collective-permute-start(f32[1,48,64]{2,1,0:T(8,128)S(1)} %get-tuple-element.23), channel_id=1, source_target_pairs={{8,0},{16,8},{24,16},{32,24},{40,32},{48,40},{56,48},{64,56},{72,6... | collective-permute-start | bytes 36872 | tf_op jit(solution)/shard_map/ppermute | solution.py:23
  204.6 108.3 %collective-permute-start.4 = (f32[1,48,64]{2,1,0:T(8,128)S(1)}, f32[1,48,64]{2,1,0:T(8,128)S(1)}, u32[]{:S(2)}, u32[]{:S(2)}) collective-permute-start(f32[1,48,64]{2,1,0:T(8,128)S(1)} %get-tuple-element.22), channel_id=1, source_target_pairs={{0,8},{8,16},{16,24},{24,32},{32,40},{40,48},{48,56},{56,64},{64,7... | collective-permute-start | bytes 36872 | tf_op jit(solution)/shard_map/ppermute | solution.py:21
  313.0 1.6 collective-permute-start.7
  313.1 5.4 collective-permute-start.6
  318.7 1.6 collective-permute-start.9
  318.8 5.4 collective-permute-start.8
  376.1 108.8 %collective-permute-start.11 = (f32[1,48,64]{2,1,0:T(8,128)S(1)}, f32[1,48,64]{2,1,0:T(8,128)S(1)}, u32[]{:S(2)}, u32[]{:S(2)}) collective-permute-start(f32[1,48,64]{2,1,0:T(8,128)S(1)} %get-tuple-element.16), channel_id=1, source_target_pairs={{8,0},{16,8},{24,16},{32,24},{40,32},{48,40},{56,48},{64,56},{72,6... | collective-permute-start | bytes 36872 | tf_op jit(solution)/shard_map/ppermute | solution.py:23
  376.2 108.8 %collective-permute-start.10 = (f32[1,48,64]{2,1,0:T(8,128)S(1)}, f32[1,48,64]{2,1,0:T(8,128)S(1)}, u32[]{:S(2)}, u32[]{:S(2)}) collective-permute-start(f32[1,48,64]{2,1,0:T(8,128)S(1)} %get-tuple-element.15), channel_id=1, source_target_pairs={{0,8},{8,16},{16,24},{24,32},{32,40},{40,48},{48,56},{56,64},{64,7... | collective-permute-start | bytes 36872 | tf_op jit(solution)/shard_map/ppermute | solution.py:21
  485.1 1.6 collective-permute-start.13
  485.2 5.4 collective-permute-start.12
  490.7 1.6 collective-permute-start.15
  490.8 5.4 collective-permute-start.14
  654.4 1.7 copy-start.8
Sparse Core Ops, SparseCore 0:
  16.1 78.8 reduce-scatter.1
where the time goes:
time: 669 us; the launch traced here: 663 us
  blocking collectives  473 us (71%)
  other arithmetic  87.4 us (13%)
  matrix products  51.3 us (8%)
  waiting for transfers between devices  21 us (3%)
  between operations  15.6 us (2%)
  starting transfers between devices  9.69 us (1%)
    psum x3, blocking collectives, body(): delta_new = lax.psum(jnp.sum(partial_value, axis=0), 'cuts') / total_slices  320 us
    all_gather x3, blocking collectives, body(): whole = lax.all_gather(tall, 'chan', axis=1, tiled=True)  111 us
    another operation x4, other arithmetic, setup_system(): factors = jax.vmap(jnp.linalg.cholesky)(system)  47.1 us
    psum x1, blocking collectives, body(): lax.psum(jnp.dot(chan_factor.T, chan_factor, preferred_element_type=jnp.f...  41.4 us
    another operation x3, other arithmetic, setup_system(): jax.scipy.linalg.cho_solve((lower, True), identity)  39.4 us
    ppermute x8, waiting for transfers between devices, with_halo(): lax.ppermute(tail, axis, [(i, (i + 1) % count) for i in range(count)])  18.9 us
  transfers between devices with their start and end apart: 17, of which 9 were waited for; matrix products, arithmetic and copies ran while one was open for 15% of the time, Pallas kernels for 0%

commit v1 on v0

--- a/solution.py
+++ b/solution.py
@@ -2,6 +2,7 @@
 import jax.numpy as jnp
 from jax import lax
 from jax.sharding import PartitionSpec as P
+from jax.lax import all_to_all, psum
 
 INNER = 3
 SWEEPS = 4
@@ -9,6 +10,18 @@
 smooth_weight = 1.0
 eps_trace = 1e-06
 highest = lax.Precision.HIGHEST
+
+
+def loads_connect(x_part, lane_axis):
+    return jnp.concatenate(
+        all_to_all(
+            jnp.stack([x_part for _ in range(psum(1, lane_axis))], axis=0),
+            axis_name=lane_axis,
+            split_axis=0,
+            concat_axis=0,
+        ),
+        1,
+    )
 
 
 def with_halo(cells, sides, width):
@@ -106,7 +119,7 @@
         target = evolving + dual_s
         aux = smooth(aux, target, rho_cols)
         tall = evolving + dual_c
-        whole = lax.all_gather(tall, "chan", axis=1, tiled=True)
+        whole = loads_connect(tall, "chan")
         gram = jnp.einsum("kir,kis->krs", whole, whole, precision=highest)
         root, scale, partial_value = polar_terms(gram, delta_now)
         delta_new = lax.psum(jnp.sum(partial_value, axis=0), "cuts") / total_slices

time: 669 us -> 623 us (0.931)
  blocking collectives: 473 us -> 374 us
  local copies, waits for them, and re-layouts: 5.17 us -> 28.5 us
  starting transfers between devices: 9.69 us -> 26 us
  other arithmetic: 87.4 us -> 95.5 us
    all_gather x3 -> x0, blocking collectives: 111 us -> none  [body(): whole = lax.all_gather(tall, 'chan', axis=1, tiled=True)]
    all_to_all x0 -> x1, blocking collectives: none -> 16.4 us  [loads_connect(): all_to_all(jnp.stack([x_part for _ in range(psum(1, lane_axis))], axis=0)...]
    unnamed x20 -> x60, local copies, waits for them, and re-layouts: 0.06 us -> 11.1 us
    reshape x0 -> x6, local copies, waits for them, and re-layouts: none -> 10.9 us  [loads_connect(): jnp.concatenate(all_to_all(jnp.stack([x_part for _ in range(psum(1, lane_...]
    all_to_all x0 -> x2, starting transfers between devices: none -> 10.2 us  [loads_connect(): all_to_all(jnp.stack([x_part for _ in range(psum(1, lane_axis))], axis=0)...]
    all_to_all x0 -> x3, other arithmetic: none -> 7.46 us  [loads_connect(): all_to_all(jnp.stack([x_part for _ in range(psum(1, lane_axis))], axis=0)...]
    all_to_all x0 -> x2, waiting for transfers between devices: none -> 7.13 us  [loads_connect(): all_to_all(jnp.stack([x_part for _ in range(psum(1, lane_axis))], axis=0)...]
  transfers between devices with their start and end apart: 17 -> 19, of which waited for: 9 -> 8; matrix products, arithmetic and copies ran while one was open for 15% -> 24% of each run, Pallas kernels for 0% -> 0%
where the time goes in v1:
time: 623 us; the launch traced here: 613 us
  blocking collectives  374 us (60%)
  other arithmetic  95.5 us (15%)
  matrix products  49.6 us (8%)
  local copies, waits for them, and re-layouts  28.5 us (5%)
  starting transfers between devices  26 us (4%)
  waiting for transfers between devices  23.5 us (4%)
  between operations  15.8 us (3%)
    psum x3, blocking collectives, body(): delta_new = lax.psum(jnp.sum(partial_value, axis=0), 'cuts') / total_slices  317 us
    another operation x4, other arithmetic, setup_system(): factors = jax.vmap(jnp.linalg.cholesky)(system)  47.1 us
    psum x1, blocking collectives, body(): lax.psum(jnp.dot(chan_factor.T, chan_factor, preferred_element_type=jnp.f...  41.4 us
    another operation x3, other arithmetic, setup_system(): jax.scipy.linalg.cho_solve((lower, True), identity)  39.4 us
    all_to_all x1, blocking collectives, loads_connect(): all_to_all(jnp.stack([x_part for _ in range(psum(1, lane_axis))], axis=0)...  16.4 us
    ppermute x8, starting transfers between devices, with_halo(): lax.ppermute(head, axis, [((i + 1) % count, i) for i in range(count)])  12.8 us
    ppermute x8, waiting for transfers between devices, with_halo(): lax.ppermute(tail, axis, [(i, (i + 1) % count) for i in range(count)])  12.7 us
  transfers between devices with their start and end apart: 19, of which 8 were waited for; matrix products, arithmetic and copies ran while one was open for 24% of the time, Pallas kernels for 0%

profile of v1, /device:TPU:8, one launch (start us, length us, event | category | flops | bytes accessed | tf_op | source)
XLA Modules:
  0.0 613.3 jit_solution(3343361535305420372)
XLA Ops:
  7.2 0.8 fusion.178
  8.0 5.2 collective-permute-start.1
  13.2 1.1 convolution_bitcast_fusion
  14.4 1.7 copy.101
  16.2 41.4 %psum.28 = f32[64,64]{1,0:T(8,128)S(1)} all-reduce(f32[64,64]{1,0:T(8,128)S(1)} %fusion.182), channel_id=1, replica_groups=mesh['cuts'=32,'chan'=8] {'chan'}, use_global_device_ids=true, to_apply=%region_1.2 | all-reduce | flops 4096 | bytes 32768 | tf_op jit(solution)/shard_map/psum | solution.py:104
  57.6 0.8 gather_fusion.1
  58.9 46.9 %custom-call.11 = f32[8,64,64]{2,1,0:T(8,128)S(1)} custom-call(f32[8,64,64]{2,1,0:T(8,128)S(1)} %add_multiply_fusion), custom_call_target="Cholesky" | custom-call | tf_op jit(solution)/shard_map/vmap(jit(cholesky))/cholesky | solution.py:50
  106.1 39.3 %custom-call.12 = f32[8,1,64,64]{2,3,1,0:T(8,128)S(1)} custom-call(f32[8,1,64,64]{3,2,1,0:T(8,128)S(1)} %select_bitcast_fusion), custom_call_target="InvertDiagBlocksLowerTriangular" | custom-call | tf_op jit(solution)/shard_map/vmap(jit(_cho_solve))/triangular_solve | solution.py:51
  146.4 1.0 copy.102
  149.1 1.0 collective-permute-done.3
  150.2 3.9 collective-permute-done.2
  155.0 1.9 reshape.121
  156.9 3.7 all-to-all-start
  160.7 3.5 collective-permute-start.7
  164.6 1.1 collective-permute-done.7
  165.7 4.7 collective-permute-done.6
  170.3 0.8 fusion.169
  172.3 3.0 all-to-all-done
  175.8 2.5 reduce.6
  178.3 1.8 reshape.122
  180.1 2.1 copy.105
  182.2 1.5 reshape.96
  183.7 2.4 fusion.183
  186.7 0.7 select_reduce_fusion.2
  197.7 105.2 %psum.29 = f32[64,64]{1,0:T(8,128)S(1)} all-reduce(f32[64,64]{1,0:T(8,128)S(1)} %fusion.24), channel_id=1, replica_groups=mesh['cuts'=32,'chan'=8] {'cuts'}, use_global_device_ids=true, to_apply=%region_7.8 | all-reduce | flops 4096 | bytes 32768 | tf_op jit(solution)/shard_map/psum | solution.py:125
  305.2 1.9 reshape.123
  307.1 6.5 %all-to-all-start.1 = ((f32[8,1,24576]{2,1,0:T(1,128)}), f32[8,1,24576]{2,1,0:T(1,128)S(1)}, u32[]{:S(2)}, u32[]{:S(2)}) async-start(f32[8,1,24576]{2,1,0:T(1,128)} %reshape.123), calls=%async_computation.2 | async-start | bytes 1572864 | tf_op jit(solution)/shard_map/all_to_all | solution.py:17
  313.7 3.8 collective-permute-start.13
  317.5 1.5 collective-permute-done.13
  319.1 4.1 collective-permute-done.12
  323.9 4.2 all-to-all-done.1
  328.1 2.5 reduce.7
  330.6 1.8 reshape.124
  332.4 2.1 copy.110
  334.5 1.5 reshape.98
  336.0 2.4 fusion.197
  349.9 105.1 %psum.30 = f32[64,64]{1,0:T(8,128)S(1)} all-reduce(f32[64,64]{1,0:T(8,128)S(1)} %fusion.25), channel_id=1, replica_groups=mesh['cuts'=32,'chan'=8] {'cuts'}, use_global_device_ids=true, to_apply=%region_10.11 | all-reduce | flops 4096 | bytes 32768 | tf_op jit(solution)/shard_map/psum | solution.py:125
  456.1 1.9 fusion.181
  458.8 1.0 reshape.125
  459.8 16.4 %all_to_all.15 = f32[8,1,24576]{2,1,0:T(1,128)S(1)} all-to-all(f32[8,1,24576]{2,1,0:T(1,128)S(1)} %reshape.125), channel_id=1, replica_groups=mesh['cuts'=32,'chan'=8] {'chan'}, dimensions={0} | all-to-all | bytes 1572864 | tf_op jit(solution)/shard_map/all_to_all | solution.py:17
  476.2 2.5 reduce.8
  478.7 1.8 reshape.126
  480.5 2.2 copy.115
  482.6 1.5 reshape.100
  484.2 2.4 fusion.211
  487.1 0.7 select_reduce_fusion
  498.0 106.3 %psum.31 = f32[64,64]{1,0:T(8,128)S(1)} all-reduce(f32[64,64]{1,0:T(8,128)S(1)} %fusion.26), channel_id=1, replica_groups=mesh['cuts'=32,'chan'=8] {'cuts'}, use_global_device_ids=true, to_apply=%region_13.14 | all-reduce | flops 4096 | bytes 32768 | tf_op jit(solution)/shard_map/psum | solution.py:125
  605.0 1.1 fusion.225
  (203 shorter events, 44.6 us)
Async XLA Ops:
  7.2 6.1 copy-start
  7.2 139.3 %reduce-scatter.2.cloned.1.call-start = ((), (), s32[]{:S(2)}) async-start(), calls=%async_computation.4 | async-start | bytes 1769472 | tf_op jit(solution)/shard_map/reduce_scatter | solution.py:96
  8.0 139.9 %collective-permute-start.1 = (f32[1,48,64]{2,1,0:T(8,128)S(1)}, f32[1,48,64]{2,1,0:T(8,128)S(1)}, u32[]{:S(2)}, u32[]{:S(2)}) collective-permute-start(f32[1,48,64]{2,1,0:T(8,128)S(1)} %get-tuple-element.28), channel_id=1, source_target_pairs={{8,0},{16,8},{24,16},{32,24},{40,32},{48,40},{56,48},{64,56},{72,6... | collective-permute-start | bytes 36872 | tf_op jit(solution)/shard_map/ppermute | solution.py:36
  13.2 134.8 %collective-permute-start = (f32[1,48,64]{2,1,0:T(8,128)S(1)}, f32[1,48,64]{2,1,0:T(8,128)S(1)}, u32[]{:S(2)}, u32[]{:S(2)}) collective-permute-start(f32[1,48,64]{2,1,0:T(8,128)S(1)} %get-tuple-element.27), channel_id=1, source_target_pairs={{0,8},{8,16},{16,24},{24,32},{32,40},{40,48},{48,56},{56,64},{64,7... | collective-permute-start | bytes 36872 | tf_op jit(solution)/shard_map/ppermute | solution.py:34
  14.3 1.7 copy-start.24
  16.0 42.4 %copy-start.23 = (f32[8,64]{1,0:T(8,128)S(1)}, f32[8,64]{1,0:T(8,128)}, u32[]{:S(2)}) copy-start(f32[8,64]{1,0:T(8,128)} %param.12) | copy-start | bytes 6148
  16.0 129.4 %copy-start.26 = (s32[8]{0:T(128)S(1)}, s32[8]{0:T(128)}, u32[]{:S(2)}) copy-start(s32[8]{0:T(128)} %param.10) | copy-start | bytes 100
  58.8 89.2 %copy-start.18 = (f32[8,48,64]{2,1,0:T(8,128)S(1)}, f32[8,48,64]{2,1,0:T(8,128)}, u32[]{:S(2)}) copy-start(f32[8,48,64]{2,1,0:T(8,128)} %param.13) | copy-start | bytes 294916
  58.8 89.2 %copy-start.20 = (f32[8,48,64]{2,1,0:T(8,128)S(1)}, f32[8,48,64]{2,1,0:T(8,128)}, u32[]{:S(2)}) copy-start(f32[8,48,64]{2,1,0:T(8,128)} %param.15) | copy-start | bytes 294916
  58.8 89.2 %copy-start.21 = (f32[8,48,64]{2,1,0:T(8,128)S(1)}, f32[8,48,64]{2,1,0:T(8,128)}, u32[]{:S(2)}) copy-start(f32[8,48,64]{2,1,0:T(8,128)} %param.16) | copy-start | bytes 294916
  58.8 89.2 %copy-start.22 = (f32[8,48,64]{2,1,0:T(8,128)S(1)}, f32[8,48,64]{2,1,0:T(8,128)}, u32[]{:S(2)}) copy-start(f32[8,48,64]{2,1,0:T(8,128)} %param.14) | copy-start | bytes 294916
  148.5 8.3 %copy-start.5 = (f32[8,48,64]{2,1,0:T(8,128)}, f32[8,48,64]{2,1,0:T(8,128)S(1)}, u32[]{:S(2)}) copy-start(f32[8,48,64]{2,1,0:T(8,128)S(1)} %get-tuple-element.26) | copy-start | bytes 294916
  148.6 1.6 collective-permute-start.3
  148.6 5.4 collective-permute-start.2
  154.2 0.7 copy-start.9
  154.2 6.3 %collective-permute-start.5 = (f32[1,48,64]{2,1,0:T(8,128)S(1)}, f32[1,48,64]{2,1,0:T(8,128)S(1)}, u32[]{:S(2)}, u32[]{:S(2)}) collective-permute-start(f32[1,48,64]{2,1,0:T(8,128)S(1)} %get-tuple-element.23), channel_id=1, source_target_pairs={{8,0},{16,8},{24,16},{32,24},{40,32},{48,40},{56,48},{64,56},{72,6... | collective-permute-start | bytes 36872 | tf_op jit(solution)/shard_map/ppermute | solution.py:36
  154.3 6.3 %collective-permute-start.4 = (f32[1,48,64]{2,1,0:T(8,128)S(1)}, f32[1,48,64]{2,1,0:T(8,128)S(1)}, u32[]{:S(2)}, u32[]{:S(2)}) collective-permute-start(f32[1,48,64]{2,1,0:T(8,128)S(1)} %get-tuple-element.22), channel_id=1, source_target_pairs={{0,8},{8,16},{16,24},{24,32},{32,40},{40,48},{48,56},{56,64},{64,7... | collective-permute-start | bytes 36872 | tf_op jit(solution)/shard_map/ppermute | solution.py:34
  156.9 3.7 copy-start.10
  156.9 18.4 %all-to-all-start = ((f32[8,1,24576]{2,1,0:T(1,128)}), f32[8,1,24576]{2,1,0:T(1,128)S(1)}, u32[]{:S(2)}, u32[]{:S(2)}) async-start(f32[8,1,24576]{2,1,0:T(1,128)} %reshape.121), calls=%async_computation.1 | async-start | bytes 1572864 | tf_op jit(solution)/shard_map/all_to_all | solution.py:17
  160.7 5.0 collective-permute-start.7
  164.2 6.2 %collective-permute-start.6 = (f32[1,48,64]{2,1,0:T(8,128)S(1)}, f32[1,48,64]{2,1,0:T(8,128)S(1)}, u32[]{:S(2)}, u32[]{:S(2)}) collective-permute-start(f32[1,48,64]{2,1,0:T(8,128)S(1)} %get-tuple-element.20), channel_id=1, source_target_pairs={{0,8},{8,16},{16,24},{24,32},{32,40},{40,48},{48,56},{56,64},{64,7... | collective-permute-start | bytes 36872 | tf_op jit(solution)/shard_map/ppermute | solution.py:34
  171.1 4.1 copy-start.13
  171.8 132.1 %collective-permute-start.9 = (f32[1,48,64]{2,1,0:T(8,128)}, f32[1,48,64]{2,1,0:T(8,128)S(1)}, u32[]{:S(2)}, u32[]{:S(2)}) collective-permute-start(f32[1,48,64]{2,1,0:T(8,128)} %get-tuple-element.19), channel_id=1, source_target_pairs={{8,0},{16,8},{24,16},{32,24},{40,32},{48,40},{56,48},{64,56},{72,6... | collective-permute-start | bytes 36872 | tf_op jit(solution)/shard_map/ppermute | solution.py:36
  171.8 132.1 %collective-permute-start.8 = (f32[1,48,64]{2,1,0:T(8,128)S(1)}, f32[1,48,64]{2,1,0:T(8,128)S(1)}, u32[]{:S(2)}, u32[]{:S(2)}) collective-permute-start(f32[1,48,64]{2,1,0:T(8,128)S(1)} %get-tuple-element.18), channel_id=1, source_target_pairs={{0,8},{8,16},{16,24},{24,32},{32,40},{40,48},{48,56},{56,64},{64,7... | collective-permute-start | bytes 36872 | tf_op jit(solution)/shard_map/ppermute | solution.py:34
  183.7 2.4 copy-start.19
  195.9 107.6 %copy-start.6 = (f32[8,48,64]{2,1,0:T(8,128)S(1)}, f32[8,48,64]{2,1,0:T(8,128)}, u32[]{:S(2)}) copy-start(f32[8,48,64]{2,1,0:T(8,128)} %copy-done.5) | copy-start | bytes 294916
  196.3 107.6 %copy-start.14 = (f32[8,48,64]{2,1,0:T(8,128)S(1)}, f32[8,48,64]{2,1,0:T(8,128)}, u32[]{:S(2)}) copy-start(f32[8,48,64]{2,1,0:T(8,128)} %copy-done.13) | copy-start | bytes 294916
  196.3 107.6 %copy-start.17 = (f32[8,48,64]{2,1,0:T(8,128)S(1)}, f32[8,48,64]{2,1,0:T(8,128)}, u32[]{:S(2)}) copy-start(f32[8,48,64]{2,1,0:T(8,128)} %get-tuple-element.5) | copy-start | bytes 294916
  304.4 0.7 copy-start.15
  304.4 2.7 copy-start.7
  304.4 18.8 %copy-start.1 = (f32[8,48,64]{2,1,0:T(8,128)}, f32[8,48,64]{2,1,0:T(8,128)S(1)}, u32[]{:S(2)}) copy-start(f32[8,48,64]{2,1,0:T(8,128)S(1)} %get-tuple-element.4) | copy-start | bytes 294916
  304.4 9.2 %collective-permute-start.11 = (f32[1,48,64]{2,1,0:T(8,128)S(1)}, f32[1,48,64]{2,1,0:T(8,128)S(1)}, u32[]{:S(2)}, u32[]{:S(2)}) collective-permute-start(f32[1,48,64]{2,1,0:T(8,128)S(1)} %get-tuple-element.16), channel_id=1, source_target_pairs={{8,0},{16,8},{24,16},{32,24},{40,32},{48,40},{56,48},{64,56},{72,6... | collective-permute-start | bytes 36872 | tf_op jit(solution)/shard_map/ppermute | solution.py:36
  304.5 9.1 %collective-permute-start.10 = (f32[1,48,64]{2,1,0:T(8,128)S(1)}, f32[1,48,64]{2,1,0:T(8,128)S(1)}, u32[]{:S(2)}, u32[]{:S(2)}) collective-permute-start(f32[1,48,64]{2,1,0:T(8,128)S(1)} %get-tuple-element.15), channel_id=1, source_target_pairs={{0,8},{8,16},{16,24},{24,32},{32,40},{40,48},{48,56},{56,64},{64,7... | collective-permute-start | bytes 36872 | tf_op jit(solution)/shard_map/ppermute | solution.py:34
  307.1 6.6 %copy-start.16 = (f32[8,48,64]{2,1,0:T(8,128)S(1)}, f32[8,48,64]{2,1,0:T(8,128)}, u32[]{:S(2)}) copy-start(f32[8,48,64]{2,1,0:T(8,128)} %copy-done.15) | copy-start | bytes 294916
  307.1 21.1 %all-to-all-start.1 = ((f32[8,1,24576]{2,1,0:T(1,128)}), f32[8,1,24576]{2,1,0:T(1,128)S(1)}, u32[]{:S(2)}, u32[]{:S(2)}) async-start(f32[8,1,24576]{2,1,0:T(1,128)} %reshape.123), calls=%async_computation.2 | async-start | bytes 1572864 | tf_op jit(solution)/shard_map/all_to_all | solution.py:17
  313.7 5.3 collective-permute-start.13
  317.5 5.6 collective-permute-start.12
  323.3 0.7 copy-start.11
  323.3 132.7 %collective-permute-start.15 = (f32[1,48,64]{2,1,0:T(8,128)S(1)}, f32[1,48,64]{2,1,0:T(8,128)S(1)}, u32[]{:S(2)}, u32[]{:S(2)}) collective-permute-start(f32[1,48,64]{2,1,0:T(8,128)S(1)} %get-tuple-element.12), channel_id=1, source_target_pairs={{8,0},{16,8},{24,16},{32,24},{40,32},{48,40},{56,48},{64,56},{72,6... | collective-permute-start | bytes 36872 | tf_op jit(solution)/shard_map/ppermute | solution.py:36
  323.4 132.7 %collective-permute-start.14 = (f32[1,48,64]{2,1,0:T(8,128)S(1)}, f32[1,48,64]{2,1,0:T(8,128)}, u32[]{:S(2)}, u32[]{:S(2)}) collective-permute-start(f32[1,48,64]{2,1,0:T(8,128)S(1)} %get-tuple-element.11), channel_id=1, source_target_pairs={{0,8},{8,16},{16,24},{24,32},{32,40},{40,48},{48,56},{56,64},{64,7... | collective-permute-start | bytes 36872 | tf_op jit(solution)/shard_map/ppermute | solution.py:34
  348.1 107.5 %copy-start.8 = (f32[8,48,64]{2,1,0:T(8,128)S(1)}, f32[8,48,64]{2,1,0:T(8,128)}, u32[]{:S(2)}) copy-start(f32[8,48,64]{2,1,0:T(8,128)} %copy-done.7) | copy-start | bytes 294916
  348.5 107.5 %copy-start.2 = (f32[8,48,64]{2,1,0:T(8,128)S(1)}, f32[8,48,64]{2,1,0:T(8,128)}, u32[]{:S(2)}) copy-start(f32[8,48,64]{2,1,0:T(8,128)} %copy-done.1) | copy-start | bytes 294916
  348.6 107.5 %copy-start.12 = (f32[8,48,64]{2,1,0:T(8,128)S(1)}, f32[8,48,64]{2,1,0:T(8,128)}, u32[]{:S(2)}) copy-start(f32[8,48,64]{2,1,0:T(8,128)} %copy-done.11) | copy-start | bytes 294916
  458.0 0.7 copy-start.3
  496.3 108.7 %copy-start.4 = (f32[8,48,64]{2,1,0:T(8,128)S(1)}, f32[8,48,64]{2,1,0:T(8,128)}, u32[]{:S(2)}) copy-start(f32[8,48,64]{2,1,0:T(8,128)} %copy-done.3) | copy-start | bytes 294916
  604.4 1.7 copy-start.25
Sparse Core Ops, SparseCore 0:
  16.2 79.0 reduce-scatter.1
